TPU v7x, 512 devices: a whole 4x8x8 slice. The times are simulated.
512 devices in a mesh: seq: 64 (over z, y), head: 8 (over x, core).
Axes of the slice: x: 4, y: 8, z: 8, core: 2. Of those that a mesh axis runs over, the one named last changes fastest.
Arguments:
- queries: bfloat16 [32768, 4096], P('seq', 'head'), may hold values from -6 to 6
- keys: bfloat16 [32768, 4096], P('seq', 'head'), may hold values from -6 to 6
- values: bfloat16 [32768, 4096], P('seq', 'head'), may hold values from -6 to 6
- decay_codes: int32 [32], P('head'), may hold values from 4 to 21
- gain: bfloat16 [4096], P('head'), may hold values from 0.099609375 to 1.8984375
- grad_out: bfloat16 [32768, 4096], P('seq', 'head'), may hold values from -6 to 6
Outputs:
- normalized: bfloat16 [32768, 4096], P('seq', 'head')
- grad_queries: bfloat16 [32768, 4096], P('seq', 'head')
- grad_keys: bfloat16 [32768, 4096], P('seq', 'head')
- grad_values: bfloat16 [32768, 4096], P('seq', 'head')
All inputs are finite; a program needn't handle non-finite values.
Results may differ from a plain program's by a relative error of at most 0.01015.
Values may be sent and summed in bfloat16 or wider, within the bound.
A program may use at most 128 MiB of HBM per device.

v0:
```python
import jax
import jax.numpy as jnp
from jax import lax
from jax.sharding import PartitionSpec as P

HEAD_DIM = 128


EPSILON = 1e-06


def entering_2(array, axis, combine, identity, reverse):
    count, here = (lax.axis_size(axis), lax.axis_index(axis))
    everything = jax.tree.map(lambda part: lax.all_gather(part, axis), array)
    start = jax.tree.map(
        lambda part, zero: jnp.broadcast_to(jnp.asarray(zero, part.dtype), part.shape),
        array,
        identity,
    )

    def turn(k, before):
        at = count - 1 - k if reverse else k
        reached = at > here if reverse else at < here
        new = combine(before, jax.tree.map(lambda part: part[at], everything))
        return jax.tree.map(lambda a, b: jnp.where(reached, a, b), new, before)

    return lax.fori_loop(0, count, turn, start)


def chain_combine(earlier, later):
    return (later[1][:, None, None] * earlier[0] + later[0], earlier[1] * later[1])


def body(queries, keys, values, decay_codes, gain, grad_out):
    tok_count = queries.shape[0]
    local_width = queries.shape[1]
    local_heads = local_width // HEAD_DIM
    features = local_width * lax.axis_size("head")
    shape3 = (tok_count, local_heads, HEAD_DIM)
    state_shape = (local_heads, HEAD_DIM, HEAD_DIM)
    query_rows = queries.reshape(shape3)
    key_rows = keys.reshape(shape3)
    value_rows = values.reshape(shape3)
    log_rates = jnp.log1p(-jnp.exp2(-decay_codes.astype(jnp.float32)))
    positions = jnp.arange(tok_count).astype(jnp.float32)
    offsets = positions[:, None] - positions[None, :]
    decay_mat = jnp.where(
        offsets[None] >= 0, jnp.exp(jnp.maximum(offsets, 0.0)[None] * log_rates[:, None, None]), 0.0
    )
    decay_near = jnp.exp(positions[:, None] * log_rates[None, :])[:, :, None]
    decay_after = jnp.exp((positions[:, None] + 1.0) * log_rates[None, :])[:, :, None]
    decay_far = jnp.exp((tok_count - 1.0 - positions)[:, None] * log_rates[None, :])[:, :, None]
    decay_lead = jnp.exp((tok_count - positions)[:, None] * log_rates[None, :])[:, :, None]
    block_pow = jnp.exp(tok_count * log_rates)
    identity = (jnp.zeros(state_shape, jnp.float32), jnp.ones((local_heads,), jnp.float32))
    decayed_keys = (key_rows * decay_lead).astype(jnp.bfloat16)
    local_state = jnp.einsum(
        "jhd,jhe->hde", decayed_keys, value_rows, preferred_element_type=jnp.float32
    )
    entering, unused_pow = entering_2(
        (local_state, block_pow), "seq", chain_combine, identity, False
    )
    entering_bf = entering.astype(jnp.bfloat16)
    scores = jnp.einsum("ihd,jhd->hij", query_rows, key_rows, preferred_element_type=jnp.float32)
    weights = (scores * decay_mat).astype(jnp.bfloat16)
    attended = jnp.einsum("hij,jhd->ihd", weights, value_rows, preferred_element_type=jnp.float32)
    attended = attended + decay_near * jnp.einsum(
        "ihd,hde->ihe", query_rows, entering_bf, preferred_element_type=jnp.float32
    )
    gain_grid = gain.astype(jnp.float32).reshape(local_heads, HEAD_DIM)
    gained_grad = gain_grid * grad_out.reshape(shape3).astype(jnp.float32)
    square_rows = jnp.sum(attended * attended, axis=(1, 2))
    square_sum = lax.psum(square_rows, "head")
    inverse_rms = lax.rsqrt(square_sum / features + EPSILON)[:, None, None]
    unit_rows = attended * inverse_rms
    normalized = unit_rows * gain_grid
    mean_term = lax.psum(jnp.sum(gained_grad * unit_rows, axis=(1, 2)), "head") / features
    grad_att = (inverse_rms * (gained_grad - unit_rows * mean_term[:, None, None])).astype(
        jnp.bfloat16
    )
    decayed_queries = (query_rows * decay_after).astype(jnp.bfloat16)
    local_back = jnp.einsum(
        "ihd,ihe->hde", decayed_queries, grad_att, preferred_element_type=jnp.float32
    )
    leaving, unused_back = entering_2((local_back, block_pow), "seq", chain_combine, identity, True)
    leaving_bf = leaving.astype(jnp.bfloat16)
    back_weights = (
        jnp.einsum("ihe,jhe->hij", grad_att, value_rows, preferred_element_type=jnp.float32)
        * decay_mat
    ).astype(jnp.bfloat16)
    grad_query = jnp.einsum(
        "hij,jhd->ihd", back_weights, key_rows, preferred_element_type=jnp.float32
    )
    grad_query = grad_query + decay_near * jnp.einsum(
        "ihe,hde->ihd", grad_att, entering_bf, preferred_element_type=jnp.float32
    )
    grad_key = jnp.einsum(
        "hij,ihd->jhd", back_weights, query_rows, preferred_element_type=jnp.float32
    )
    grad_key = grad_key + decay_far * jnp.einsum(
        "jhe,hde->jhd", value_rows, leaving_bf, preferred_element_type=jnp.float32
    )
    grad_value = jnp.einsum("hij,ihe->jhe", weights, grad_att, preferred_element_type=jnp.float32)
    grad_value = grad_value + decay_far * jnp.einsum(
        "jhd,hde->jhe", key_rows, leaving_bf, preferred_element_type=jnp.float32
    )
    flat = (tok_count, local_width)
    return (
        normalized.astype(jnp.bfloat16).reshape(flat),
        grad_query.astype(jnp.bfloat16).reshape(flat),
        grad_key.astype(jnp.bfloat16).reshape(flat),
        grad_value.astype(jnp.bfloat16).reshape(flat),
    )


def solution(mesh):
    in_specs = (
        P("seq", "head"),
        P("seq", "head"),
        P("seq", "head"),
        P("head"),
        P("head"),
        P("seq", "head"),
    )
    out_specs = (P("seq", "head"), P("seq", "head"), P("seq", "head"), P("seq", "head"))
    return jax.shard_map(body, mesh=mesh, in_specs=in_specs, out_specs=out_specs, check_vma=False)
```

profile of v0, /device:TPU:1, one launch (start us, length us, event | category | flops | bytes accessed | tf_op | source)
XLA Modules:
  0.0 484.3 jit_solution(13825909970411360956)
XLA Ops:
  7.3 1.4 copy.108
  8.7 1.3 dynamic-slice
  12.6 127.4 %all-reduce = f32[256]{0:T(256)S(1)} all-reduce(f32[256]{0:T(256)S(1)} %get-tuple-element.306), channel_id=2, replica_groups=mesh['seq'=64,'head'=8] {'seq'}, use_global_device_ids=true, to_apply=%add | all-reduce | flops 256 | bytes 2048
  140.2 1.3 copy.81
  142.1 1.4 multiply_convert_fusion.1
  143.6 1.3 copy-done.1
  144.9 1.8 convolution_bitcast_fusion.3
  146.7 12.5 %all-gather.6.cloned.1.call-done = f32[256,128,128]{2,1,0:T(8,128)} async-done(((f32[4,128,128]{2,1,0:T(8,128)}), f32[256,128,128]{2,1,0:T(8,128)}) %all-gather.6.cloned.1.call-update) | async-done | bytes 16777232 | tf_op jit(solution)/shard_map/all_gather | solution.py:14
  159.3 70.2 %while.30 = (s32[]{:T(128)}, f32[4,128,128]{2,1,0:T(8,128)S(1)}, s32[]{:T(128)}, f32[64,4]{1,0:T(8,128)S(1)}, f32[64,4,128,128]{3,2,1,0:T(8,128)}, /*index=5*/s32[]{:T(128)}, s32[]{:T(128)}) while((s32[]{:T(128)}, f32[4,128,128]{2,1,0:T(8,128)S(1)}, s32[]{:T(128)}, f32[64,4]{1,0:T(8,128)S(1)}, f32[64,4,128,128]{3,2,1,0:T(8,128)}, ...), condition=%wide.region_1.2_spmd.clone, body=%wide.region_0.1_spmd.clone.sunk | while | flops 262148 | bytes 786593 | solution.py:27
  229.5 1.6 multiply_reduce_fusion.1
  231.1 27.1 %psum.14 = f32[512]{0:T(512)S(1)} all-reduce(f32[512]{0:T(512)S(1)} %get-tuple-element.308), channel_id=1, replica_groups=mesh['seq'=64,'head'=8] {'head'}, use_global_device_ids=true, to_apply=%region_3.4 | all-reduce | flops 512 | bytes 4096 | tf_op jit(solution)/shard_map/psum | solution.py:73
  258.4 12.3 %psum.15 = f32[512]{0:T(512)S(1)} all-reduce(f32[512]{0:T(512)S(1)} %multiply_reduce_fusion), channel_id=1, replica_groups=mesh['seq'=64,'head'=8] {'head'}, use_global_device_ids=true, to_apply=%region_5.6 | all-reduce | flops 512 | bytes 4096 | tf_op jit(solution)/shard_map/psum | solution.py:77
  270.7 1.1 multiply_convert_fusion.3
  273.6 2.0 copy.72
  275.7 2.9 multiply_convert_fusion
  278.6 2.4 convolution_bitcast_fusion.2
  281.0 1.1 fusion.10
  282.1 2.0 copy.73
  284.1 2.6 convolution_bitcast_fusion.1
  286.8 1.6 convolution_bitcast_fusion
  288.4 112.9 %all-gather.8.cloned.1.call-done = f32[256,128,128]{2,1,0:T(8,128)} async-done(((f32[4,128,128]{2,1,0:T(8,128)}), f32[256,128,128]{2,1,0:T(8,128)}) %all-gather.8.cloned.1.call-update) | async-done | bytes 16777232 | tf_op jit(solution)/shard_map/all_gather | solution.py:14
  401.3 70.6 %while.31 = (s32[]{:T(128)}, f32[4,128,128]{2,1,0:T(8,128)S(1)}, s32[]{:T(128)}, f32[64,4]{1,0:T(8,128)S(1)}, f32[64,4,128,128]{3,2,1,0:T(8,128)}, /*index=5*/s32[]{:T(128)}, s32[]{:T(128)}, s32[]{:T(128)}, s32[]{:T(128)}) while((s32[]{:T(128)}, f32[4,128,128]{2,1,0:T(8,128)S(1)}, s32[]{:T(128)}, f32[64,4]{1,0:T(8,128)S(1)}, ...), condition=%wide.region_7.8_spmd.clone, body=%wide.region_6.7_spmd.clone.sunk | while | flops 262152 | bytes 786655 | solution.py:27
  471.9 2.2 fusion.12
  474.1 2.0 copy.75
  (309 shorter events, 142.4 us)
Async XLA Ops:
  7.2 4.4 copy-start
  7.2 134.9 %copy-start.10 = (bf16[512,512]{1,0:T(8,128)(2,1)S(1)}, bf16[512,512]{1,0:T(8,128)(2,1)}, u32[]{:S(2)}) copy-start(bf16[512,512]{1,0:T(8,128)(2,1)} %param.11) | copy-start | bytes 1572868
  7.2 134.3 %copy-start.12 = (bf16[512,512]{1,0:T(8,128)(2,1)S(1)}, bf16[512,512]{1,0:T(8,128)(2,1)}, u32[]{:S(2)}) copy-start(bf16[512,512]{1,0:T(8,128)(2,1)} %param.15) | copy-start | bytes 1572868
  7.2 134.5 %copy-start.14 = (bf16[512]{0:T(512)(128)(2,1)S(1)}, bf16[512]{0:T(512)(128)(2,1)}, u32[]{:S(2)}) copy-start(bf16[512]{0:T(512)(128)(2,1)} %param.14) | copy-start | bytes 3076
  7.2 152.0 %all-gather.6.cloned.1.call-start = ((), (), s32[]{:S(2)}) async-start(), calls=%async_computation | async-start | bytes 17039360 | tf_op jit(solution)/shard_map/all_gather | solution.py:14
  8.7 3.9 copy-start.9
  12.6 388.7 %all-gather.8.cloned.1.call-start = ((), (), s32[]{:S(2)}) async-start(), calls=%async_computation.1 | async-start | bytes 17039360 | tf_op jit(solution)/shard_map/all_gather | solution.py:14
  141.5 130.3 %copy-start.5 = (bf16[512,512]{0,1:T(8,128)(2,1)}, bf16[512,512]{0,1:T(8,128)(2,1)S(1)}, u32[]{:S(2)}) copy-start(bf16[512,512]{0,1:T(8,128)(2,1)S(1)} %copy.81) | copy-start | bytes 1572868
  142.0 1.6 copy-start.13
  142.1 1.5 copy-start.11
  143.6 1.3 copy-start.1
  271.8 0.8 copy-start.6
  275.7 5.3 %copy-start.7 = (bf16[512,4,128]{0,2,1:T(8,128)(2,1)S(1)}, bf16[512,4,128]{0,2,1:T(8,128)(2,1)}, u32[]{:S(2)}) copy-start(bf16[512,4,128]{0,2,1:T(8,128)(2,1)} %copy-done.6) | copy-start | bytes 1572868
  278.6 3.5 copy-start.3
  278.6 5.6 %copy-start.2 = (bf16[4,512,512]{2,1,0:T(8,128)(2,1)S(1)}, bf16[4,512,512]{2,1,0:T(8,128)(2,1)}, u32[]{:S(2)}) copy-start(bf16[4,512,512]{2,1,0:T(8,128)(2,1)} %copy-done.1) | copy-start | bytes 6291460
  284.1 2.6 copy-start.4
  286.8 185.1 %copy-start.8 = (f32[512,4,128]{0,2,1:T(8,128)S(1)}, f32[512,4,128]{0,2,1:T(8,128)}, u32[]{:S(2)}) copy-start(f32[512,4,128]{0,2,1:T(8,128)} %convolution_bitcast_fusion.1) | copy-start | bytes 3145732
Sparse Core Ops, SparseCore 0:
  12.7 146.5 all-gather.5
  273.7 127.5 all-gather.7
where the time goes:
time: 489 us; the launch traced here: 484 us
  blocking collectives  167 us (34%)
  other arithmetic  138 us (28%)
  waiting for transfers between devices  125 us (26%)
  matrix products  19.9 us (4%)
  between operations  15 us (3%)
  local copies, waits for them, and re-layouts  14.8 us (3%)
    select_n x128, other arithmetic, turn(): return jax.tree.map(lambda a, b: jnp.where(reached, a, b), new, before)  135 us
    unnamed x1, blocking collectives  127 us
    all_gather x2, waiting for transfers between devices, entering_2(): everything = jax.tree.map(lambda part: lax.all_gather(part, axis), array)  125 us
    psum x1, blocking collectives, body(): square_sum = lax.psum(square_rows, 'head')  27.1 us
    psum x1, blocking collectives, body(): lax.psum(jnp.sum(gained_grad * unit_rows, axis=(1, 2)), 'head') / features  12.3 us
    unnamed x36, local copies, waits for them, and re-layouts  10.6 us
  transfers between devices with their start and end apart: 2, of which 2 were waited for; matrix products, arithmetic and copies ran while one was open for 4% of the time, Pallas kernels for 0%

commit v1 on v0

v1 whole, which is shorter than its diff:
```python
import functools

import jax
import jax.numpy as jnp
from jax import lax
from jax.experimental import pallas as pl
from jax.experimental.pallas import tpu as pltpu
from jax.sharding import PartitionSpec as P

HEAD_DIM = 128
EPSILON = 1e-06
ROW = 8
HALF = 256
F32 = jnp.float32
BF16 = jnp.bfloat16
MESH = pl.DeviceIdType.MESH


def dot(a, b, ca, cb):
    return lax.dot_general(a, b, (((ca,), (cb,)), ((), ())), preferred_element_type=F32)


def kernel(
    row, planes, peers,
    codes_ref, q_ref, k_ref, v_ref, gain_ref, go_ref,
    norm_ref, gq_ref, gk_ref, gv_ref,
    decay_ref, w_ref, att_ref, gg_ref, ga_ref, dq_ref, acck_ref, accv_ref,
    state_ref, row_recv, pre_ref, tot_ref, plane_recv, full_ref, back_recv,
    part_ref, peer_recv,
    row_send, row_sem, plane_send, plane_sem, back_send, back_sem, peer_send, peer_sem,
):
    tok, width = q_ref.shape
    heads = width // HEAD_DIM
    part_rows = HEAD_DIM // row
    seq = lax.axis_index("seq")
    me = lax.axis_index("head")
    z, y = seq // row, lax.rem(seq, row)

    def row_peer(o):
        return lax.rem(y + o, row)

    barrier = pltpu.get_barrier_semaphore()
    for o in range(1, row):
        pl.semaphore_signal(
            barrier, inc=1, device_id=(z * row + row_peer(o), me), device_id_type=MESH
        )
    for o in range(1, planes):
        pl.semaphore_signal(
            barrier, inc=1, device_id=(lax.rem(z + o, planes) * row + y, me), device_id_type=MESH
        )
    for o in range(1, peers):
        pl.semaphore_signal(
            barrier, inc=1, device_id=(seq, lax.rem(me + o, peers)), device_id_type=MESH
        )

    def lanes(h):
        return slice(h * HEAD_DIM, (h + 1) * HEAD_DIM)

    rates = []
    for h in range(heads):
        code = jnp.full((8, HALF), codes_ref[h], jnp.int32).astype(F32)
        rates.append(jnp.log1p(-jnp.exp2(-code)))

    positions = lax.broadcasted_iota(jnp.int32, (tok, HEAD_DIM), 0).astype(F32)

    def powers(h, exponent):
        return jnp.exp(exponent * rates[h][0:1, :HEAD_DIM])

    def power(h, n):
        return jnp.exp(F32(n) * rates[h][0:1, :HEAD_DIM])

    def row_copy(s, o):
        return pltpu.make_async_remote_copy(
            src_ref=state_ref.at[s, row_peer(o)],
            dst_ref=row_recv.at[s, y],
            send_sem=row_send.at[s, o],
            recv_sem=row_sem.at[s, o],
            device_id=(z * row + row_peer(o), me),
            device_id_type=MESH,
        )

    def plane_copy(s, o):
        to = z + o if s == 0 else z - o
        return pltpu.make_async_remote_copy(
            src_ref=tot_ref.at[s],
            dst_ref=plane_recv.at[s, z],
            send_sem=plane_send.at[s, o],
            recv_sem=plane_sem.at[s, o],
            device_id=(lax.rem(to + planes, planes) * row + y, me),
            device_id_type=MESH,
        )

    def back_copy(s, o):
        return pltpu.make_async_remote_copy(
            src_ref=full_ref.at[s, row_peer(o)],
            dst_ref=back_recv.at[s, y],
            send_sem=back_send.at[s, o],
            recv_sem=back_sem.at[s, o],
            device_id=(z * row + row_peer(o), me),
            device_id_type=MESH,
        )

    def sends_plane(s, o):
        return z + o < planes if s == 0 else z - o >= 0

    def takes_plane(s, o):
        return z - o >= 0 if s == 0 else z + o < planes

    def put_state(s, h, value):
        state_ref[s, :, h] = value.astype(BF16).reshape(row, part_rows, HEAD_DIM)

    def start_row(s):
        for o in range(1, row):
            row_copy(s, o).start()
        row_recv[s, y] = state_ref[s, y]

    def turn_row(s):
        for o in range(1, row):
            row_copy(s, o).wait_recv()
        for h in range(heads):
            step = power(h, tok)
            held = jnp.zeros((part_rows, HEAD_DIM), F32)
            for c in range(row) if s == 0 else reversed(range(row)):
                pre_ref[s, c, h] = held
                held = step * held + row_recv[s, c, h].astype(F32)
            tot_ref[s, h] = held.astype(BF16)
        for o in range(1, planes):
            @pl.when(sends_plane(s, o))
            def _():
                plane_copy(s, o).start()

    def turn_plane(s):
        for o in range(1, planes):
            @pl.when(takes_plane(s, o))
            def _():
                plane_copy(s, o).wait_recv()
        zero = tuple(jnp.zeros((part_rows, HEAD_DIM), F32) for _ in range(heads))
        leap = [power(h, tok * row) for h in range(heads)]

        def add(t, held):
            at = t if s == 0 else planes - 1 - t
            return tuple(
                leap[h] * held[h] + plane_recv[s, at, h].astype(F32) for h in range(heads)
            )

        held = lax.fori_loop(0, z if s == 0 else planes - 1 - z, add, zero)
        for h in range(heads):
            for c in range(row):
                far = c if s == 0 else row - 1 - c
                full_ref[s, c, h] = (pre_ref[s, c, h] + power(h, tok * far) * held[h]).astype(BF16)
        for o in range(1, row):
            back_copy(s, o).start()
        back_recv[s, y] = full_ref[s, y]

    def end_scan(s):
        for o in range(1, row):
            back_copy(s, o).wait_recv()

    def crossing(s, h):
        return back_recv[s, :, h].reshape(HEAD_DIM, HEAD_DIM)

    for h in range(heads):
        lead = powers(h, F32(tok) - positions)
        decayed = (k_ref[:, lanes(h)].astype(F32) * lead).astype(BF16)
        put_state(0, h, dot(decayed, v_ref[:, lanes(h)], 0, 0))

    pl.semaphore_wait(barrier, row + planes + peers - 3)
    start_row(0)

    halves = tok // HALF
    blocks = [(r, c) for r in range(halves) for c in range(r + 1)]

    def rows_of(r):
        return slice(r * HALF, (r + 1) * HALF)

    def local_forward(h):
        at = lanes(h)
        offset = (
            lax.broadcasted_iota(jnp.int32, (HALF, HALF), 0)
            - lax.broadcasted_iota(jnp.int32, (HALF, HALF), 1)
        ).astype(F32)
        rate = rates[h][0:1, :]
        for d in range(halves):
            away = offset + F32(d * HALF)
            value = jnp.exp(jnp.maximum(away, 0.0) * rate)
            if d == 0:
                value = jnp.where(away >= 0, value, 0.0)
            decay_ref[h, d] = value
        for r in range(halves):
            total = None
            for c in range(r + 1):
                scores = dot(q_ref[rows_of(r), at], k_ref[rows_of(c), at], 1, 1)
                weights = (scores * decay_ref[h, r - c]).astype(BF16)
                w_ref[h, blocks.index((r, c))] = weights
                term = dot(weights, v_ref[rows_of(c), at], 1, 0)
                total = term if total is None else total + term
            att_ref[rows_of(r), at] = total
        after = powers(h, positions + 1.0)
        dq_ref[:, at] = (q_ref[:, at].astype(F32) * after).astype(BF16)
        gg_ref[:, at] = gain_ref[0:1, at].astype(F32) * go_ref[:, at].astype(F32)

    local_forward(0)
    local_forward(1)
    turn_row(0)
    local_forward(2)
    turn_plane(0)
    local_forward(3)
    end_scan(0)

    squares = jnp.zeros((tok, HEAD_DIM), F32)
    crosses = jnp.zeros((tok, HEAD_DIM), F32)
    for h in range(heads):
        at = lanes(h)
        near = powers(h, positions)
        att = att_ref[:, at] + near * dot(q_ref[:, at], crossing(0, h), 1, 0)
        att_ref[:, at] = att
        squares = squares + att * att
        crosses = crosses + gg_ref[:, at] * att
    part_ref[0:1, :] = jnp.sum(squares.T, axis=0, keepdims=True)
    part_ref[1:2, :] = jnp.sum(crosses.T, axis=0, keepdims=True)

    def peer_copy(o):
        return pltpu.make_async_remote_copy(
            src_ref=part_ref,
            dst_ref=peer_recv.at[me],
            send_sem=peer_send.at[o],
            recv_sem=peer_sem.at[o],
            device_id=(seq, lax.rem(me + o, peers)),
            device_id_type=MESH,
        )

    for o in range(1, peers):
        peer_copy(o).start()
    peer_recv[me] = part_ref[...]
    for o in range(1, peers):
        peer_copy(o).wait_recv()
    sums = peer_recv[0]
    for p in range(1, peers):
        sums = sums + peer_recv[p]
    features = F32(width * peers)
    inverse_row = lax.rsqrt(sums[0:1, :] / features + EPSILON)
    mean_row = inverse_row * sums[1:2, :] / features
    inverse = jnp.broadcast_to(inverse_row, (HEAD_DIM, tok)).T
    mean = jnp.broadcast_to(mean_row, (HEAD_DIM, tok)).T

    for h in range(heads):
        at = lanes(h)
        unit = att_ref[:, at] * inverse
        norm_ref[:, at] = (unit * gain_ref[0:1, at].astype(F32)).astype(BF16)
        grad = (inverse * (gg_ref[:, at] - unit * mean)).astype(BF16)
        ga_ref[:, at] = grad
        put_state(1, h, dot(dq_ref[:, at], grad, 0, 0))
    start_row(1)

    def local_backward(h):
        at = lanes(h)
        to_q = [None] * halves
        to_k = [None] * halves
        to_v = [None] * halves

        def add(old, new):
            return new if old is None else old + new

        for r, c in blocks:
            grad = ga_ref[rows_of(r), at]
            back = dot(grad, v_ref[rows_of(c), at], 1, 1)
            back = (back * decay_ref[h, r - c]).astype(BF16)
            to_q[r] = add(to_q[r], dot(back, k_ref[rows_of(c), at], 1, 0))
            to_k[c] = add(to_k[c], dot(back, q_ref[rows_of(r), at], 0, 0))
            to_v[c] = add(to_v[c], dot(w_ref[h, blocks.index((r, c))], grad, 0, 0))
        for r in range(halves):
            near = powers(h, positions[rows_of(r), :])
            grad = ga_ref[rows_of(r), at]
            gq_ref[rows_of(r), at] = (
                to_q[r] + near * dot(grad, crossing(0, h), 1, 1)
            ).astype(BF16)
            acck_ref[rows_of(r), at] = to_k[r]
            accv_ref[rows_of(r), at] = to_v[r]

    local_backward(0)
    local_backward(1)
    turn_row(1)
    local_backward(2)
    turn_plane(1)
    local_backward(3)
    end_scan(1)

    for h in range(heads):
        at = lanes(h)
        far = powers(h, F32(tok - 1) - positions)
        left = crossing(1, h)
        gk_ref[:, at] = (acck_ref[:, at] + far * dot(v_ref[:, at], left, 1, 1)).astype(BF16)
        gv_ref[:, at] = (accv_ref[:, at] + far * dot(k_ref[:, at], left, 1, 0)).astype(BF16)

    for s in range(2):
        for o in range(1, row):
            row_copy(s, o).wait_send()
            back_copy(s, o).wait_send()
        for o in range(1, planes):
            @pl.when(sends_plane(s, o))
            def _():
                plane_copy(s, o).wait_send()
    for o in range(1, peers):
        peer_copy(o).wait_send()


def body(row, planes, peers, queries, keys, values, decay_codes, gain, grad_out):
    tok, width = queries.shape
    heads = width // HEAD_DIM
    part_rows = HEAD_DIM // row
    halves = tok // HALF
    slices = (heads, part_rows, HEAD_DIM)
    vmem = pl.BlockSpec(memory_space=pltpu.VMEM)
    out = jax.ShapeDtypeStruct((tok, width), BF16)
    wide = pltpu.VMEM((tok, width), F32)
    thin = pltpu.VMEM((tok, width), BF16)
    return pl.pallas_call(
        functools.partial(kernel, row, planes, peers),
        out_shape=(out,) * 4,
        in_specs=[pl.BlockSpec(memory_space=pltpu.SMEM)] + [vmem] * 5,
        out_specs=(vmem,) * 4,
        scratch_shapes=[
            pltpu.VMEM((heads, halves, HALF, HALF), F32),
            pltpu.VMEM((heads, halves * (halves + 1) // 2, HALF, HALF), BF16),
            wide, wide, thin, thin, wide, wide,
            pltpu.VMEM((2, row) + slices, BF16),
            pltpu.VMEM((2, row) + slices, BF16),
            pltpu.VMEM((2, row) + slices, F32),
            pltpu.VMEM((2,) + slices, BF16),
            pltpu.VMEM((2, planes) + slices, BF16),
            pltpu.VMEM((2, row) + slices, BF16),
            pltpu.VMEM((2, row) + slices, BF16),
            pltpu.VMEM((2, tok), F32),
            pltpu.VMEM((peers, 2, tok), F32),
            pltpu.SemaphoreType.DMA((2, row)),
            pltpu.SemaphoreType.DMA((2, row)),
            pltpu.SemaphoreType.DMA((2, planes)),
            pltpu.SemaphoreType.DMA((2, planes)),
            pltpu.SemaphoreType.DMA((2, row)),
            pltpu.SemaphoreType.DMA((2, row)),
            pltpu.SemaphoreType.DMA((peers,)),
            pltpu.SemaphoreType.DMA((peers,)),
        ],
        compiler_params=pltpu.CompilerParams(
            collective_id=0, has_side_effects=True, vmem_limit_bytes=56 * 1024 * 1024
        ),
        name="lightning",
    )(decay_codes, queries, keys, values, gain.reshape(1, width), grad_out)


def solution(mesh):
    split = P("seq", "head")
    planes = mesh.shape["seq"] // ROW
    return jax.shard_map(
        functools.partial(body, ROW, planes, mesh.shape["head"]),
        mesh=mesh,
        in_specs=(split, split, split, P("head"), P("head"), split),
        out_specs=(split,) * 4,
        check_vma=False,
    )
```

time: 489 us -> 63.3 us (0.13)
  the two profiles are of different devices: /device:TPU:1 before, /device:TPU:16 now
where the time goes in v1:
time: 63.3 us; the launch traced here: 63 us
  Pallas kernels  55.9 us (88%)
  local copies, waits for them, and re-layouts  6.44 us (10%)
  between operations  0.65 us (1%)
    pallas_call x1, Pallas kernels, body(): pl.pallas_call(functools.partial(kernel, row, planes, peers), out_shape=(...  55.9 us
    unnamed x10, local copies, waits for them, and re-layouts  5.18 us

profile of v1, /device:TPU:16, one launch (start us, length us, event | category | flops | bytes accessed | tf_op | source)
XLA Modules:
  0.0 63.0 jit_solution(14441943508777775520)
XLA Ops:
  0.6 1.3 %reshape.11.gain_ref = bf16[1,512]{1,0:T(2,128)(2,1)} reshape(bf16[512]{0:T(512)(128)(2,1)} %param.10) | data formatting | bytes 2048 | tf_op jit(solution)/shard_map/reshape | solution.py:348
  1.9 55.9 %lightning.1 = (bf16[512,512]{1,0:T(8,128)(2,1)}, bf16[512,512]{1,0:T(8,128)(2,1)}, bf16[512,512]{1,0:T(8,128)(2,1)}, bf16[512,512]{1,0:T(8,128)(2,1)}) custom-call(s32[4]{0:T(128)} %codes_ref.1, bf16[512,512]{1,0:T(8,128)(2,1)} %q_ref.1, bf16[512,512]{1,0:T(8,128)(2,1)} %k_ref.1, bf16[512,512]{1,0:T(8,128)(2,1)} %v_ref.1, bf16[1,512]{1,0:T(2,128)(2,1)} %reshape.11.gain_ref, ...), custom_call_target="tpu_custom_call" | custom-call | tf_op jit(solution)/shard_map/lightning/pallas_call | solution.py:317
  57.8 0.0 copy-start.2
  57.8 1.9 %copy.14 = bf16[512,512]{1,0:T(8,128)(2,1)} copy(bf16[512,512]{1,0:T(8,128)(2,1)} %get-tuple-element.8) | data formatting | bytes 1048576
  59.7 0.0 copy-done.2
  59.7 0.0 copy-start.1
  59.7 0.8 %copy.15 = bf16[512,512]{1,0:T(8,128)(2,1)} copy(bf16[512,512]{1,0:T(8,128)(2,1)S(1)} %copy-done.2) | data formatting | bytes 1048576
  60.5 0.4 copy-done.1
  60.9 0.0 copy-start
  60.9 0.8 %copy.16 = bf16[512,512]{1,0:T(8,128)(2,1)} copy(bf16[512,512]{1,0:T(8,128)(2,1)S(1)} %copy-done.1) | data formatting | bytes 1048576
  61.7 0.4 copy-done
  62.2 0.8 %copy.17 = bf16[512,512]{1,0:T(8,128)(2,1)} copy(bf16[512,512]{1,0:T(8,128)(2,1)S(1)} %copy-done) | data formatting | bytes 1048576
Async XLA Ops:
  57.8 1.9 %copy-start.2 = (bf16[512,512]{1,0:T(8,128)(2,1)S(1)}, bf16[512,512]{1,0:T(8,128)(2,1)}, u32[]{:S(2)}) copy-start(bf16[512,512]{1,0:T(8,128)(2,1)} %get-tuple-element.9) | copy-start | bytes 1572868
  59.7 1.2 %copy-start.1 = (bf16[512,512]{1,0:T(8,128)(2,1)S(1)}, bf16[512,512]{1,0:T(8,128)(2,1)}, u32[]{:S(2)}) copy-start(bf16[512,512]{1,0:T(8,128)(2,1)} %get-tuple-element.10) | copy-start | bytes 1572868
  60.9 1.2 %copy-start = (bf16[512,512]{1,0:T(8,128)(2,1)S(1)}, bf16[512,512]{1,0:T(8,128)(2,1)}, u32[]{:S(2)}) copy-start(bf16[512,512]{1,0:T(8,128)(2,1)} %get-tuple-element.11) | copy-start | bytes 1572868

commit v2 on v1

v2 whole, which is shorter than its diff:
```python
import functools

import jax
import jax.numpy as jnp
from jax import lax
from jax.experimental import pallas as pl
from jax.experimental.pallas import tpu as pltpu
from jax.sharding import PartitionSpec as P

HEAD_DIM = 128
EPSILON = 1e-06
ROW = 8
HALF = 256
GROUPS = 2
VMEM_A = 67043328
VMEM_B = 67043328
F32 = jnp.float32
BF16 = jnp.bfloat16
MESH = pl.DeviceIdType.MESH


def dot(a, b, ca, cb):
    return lax.dot_general(a, b, (((ca,), (cb,)), ((), ())), preferred_element_type=F32)


def kernel(
    row, planes, peers,
    codes_hbm, q_hbm, k_hbm, v_hbm, gain_hbm, go_hbm,
    norm_out, gq_out, acck_out, accv_out, left_ref,
    codes_ref, gain_ref, q_ref, k_ref, v_ref, go_ref, norm_ref, gq_ref, acck_ref, accv_ref,
    decay_ref, w_ref, att_ref, gg_ref, ga_ref, dq_ref, near_ref,
    state_ref, row_recv, pre_ref, tot_ref, plane_recv, full_ref, back_recv,
    part_ref, peer_recv, load_sem, store_sem,
    row_send, row_sem, plane_send, plane_sem, back_send, back_sem, peer_send, peer_sem,
):
    tok, width = q_ref.shape
    heads = width // HEAD_DIM
    part_rows = HEAD_DIM // row
    team = heads // GROUPS
    seq = lax.axis_index("seq")
    me = lax.axis_index("head")
    z, y = seq // row, lax.rem(seq, row)

    def row_peer(o):
        return lax.rem(y + o, row)

    sources = (
        (codes_hbm, codes_ref), (k_hbm, k_ref), (v_hbm, v_ref),
        (q_hbm, q_ref), (gain_hbm, gain_ref), (go_hbm, go_ref),
    )
    results = ((norm_ref, norm_out), (gq_ref, gq_out), (acck_ref, acck_out), (accv_ref, accv_out))

    def load(n):
        return pltpu.make_async_copy(*sources[n], load_sem.at[n])

    def store(n):
        return pltpu.make_async_copy(*results[n], store_sem.at[n])

    for n in range(6):
        load(n).start()

    barrier = pltpu.get_barrier_semaphore()
    for o in range(1, row):
        pl.semaphore_signal(
            barrier, inc=1, device_id=(z * row + row_peer(o), me), device_id_type=MESH
        )
    for o in range(1, planes):
        pl.semaphore_signal(
            barrier, inc=1, device_id=(lax.rem(z + o, planes) * row + y, me), device_id_type=MESH
        )
    for o in range(1, peers):
        pl.semaphore_signal(
            barrier, inc=1, device_id=(seq, lax.rem(me + o, peers)), device_id_type=MESH
        )

    def lanes(h):
        return slice(h * HEAD_DIM, (h + 1) * HEAD_DIM)

    load(0).wait()
    rates = []
    for h in range(heads):
        code = jnp.full((8, HALF), codes_ref[h], jnp.int32).astype(F32)
        rates.append(jnp.log1p(-jnp.exp2(-code)))

    positions = lax.broadcasted_iota(jnp.int32, (tok, HEAD_DIM), 0).astype(F32)

    def powers(h, exponent):
        return jnp.exp(exponent * rates[h][0:1, :HEAD_DIM])

    def power(h, n):
        return jnp.exp(F32(n) * rates[h][0:1, :HEAD_DIM])

    def row_copy(s, g, o):
        return pltpu.make_async_remote_copy(
            src_ref=state_ref.at[s, g, row_peer(o)],
            dst_ref=row_recv.at[s, g, y],
            send_sem=row_send.at[s * GROUPS + g, o],
            recv_sem=row_sem.at[s * GROUPS + g, o],
            device_id=(z * row + row_peer(o), me),
            device_id_type=MESH,
        )

    def plane_copy(s, g, o):
        to = z + o if s == 0 else z - o
        return pltpu.make_async_remote_copy(
            src_ref=tot_ref.at[s, g],
            dst_ref=plane_recv.at[s, g, z],
            send_sem=plane_send.at[s * GROUPS + g, o],
            recv_sem=plane_sem.at[s * GROUPS + g, o],
            device_id=(lax.rem(to + planes, planes) * row + y, me),
            device_id_type=MESH,
        )

    def back_copy(s, g, o):
        return pltpu.make_async_remote_copy(
            src_ref=full_ref.at[s, g, row_peer(o)],
            dst_ref=back_recv.at[s, g, y],
            send_sem=back_send.at[s * GROUPS + g, o],
            recv_sem=back_sem.at[s * GROUPS + g, o],
            device_id=(z * row + row_peer(o), me),
            device_id_type=MESH,
        )

    def sends_plane(s, o):
        return z + o < planes if s == 0 else z - o >= 0

    def takes_plane(s, o):
        return z - o >= 0 if s == 0 else z + o < planes

    def put_state(s, h, value):
        g, t = divmod(h, team)
        state_ref[s, g, :, t] = value.astype(BF16).reshape(row, part_rows, HEAD_DIM)

    def start_row(s, g):
        for o in range(1, row):
            row_copy(s, g, o).start()
        row_recv[s, g, y] = state_ref[s, g, y]

    def turn_row(s, g):
        for o in range(1, row):
            row_copy(s, g, o).wait_recv()
        for t in range(team):
            step = power(g * team + t, tok)
            held = jnp.zeros((part_rows, HEAD_DIM), F32)
            for c in range(row) if s == 0 else reversed(range(row)):
                pre_ref[s, g, c, t] = held
                held = step * held + row_recv[s, g, c, t].astype(F32)
            tot_ref[s, g, t] = held.astype(BF16)
        for o in range(1, planes):
            @pl.when(sends_plane(s, o))
            def _():
                plane_copy(s, g, o).start()

    def turn_plane(s, g):
        for o in range(1, planes):
            @pl.when(takes_plane(s, o))
            def _():
                plane_copy(s, g, o).wait_recv()
        zero = tuple(jnp.zeros((part_rows, HEAD_DIM), F32) for _ in range(team))
        leap = [power(g * team + t, tok * row) for t in range(team)]

        def add(n, held):
            at = n if s == 0 else planes - 1 - n
            return tuple(
                leap[t] * held[t] + plane_recv[s, g, at, t].astype(F32) for t in range(team)
            )

        held = lax.fori_loop(0, z if s == 0 else planes - 1 - z, add, zero)
        for t in range(team):
            for c in range(row):
                far = power(g * team + t, tok * (c if s == 0 else row - 1 - c))
                full_ref[s, g, c, t] = (pre_ref[s, g, c, t] + far * held[t]).astype(BF16)
        for o in range(1, row):
            back_copy(s, g, o).start()
        back_recv[s, g, y] = full_ref[s, g, y]

    def end_scan(s, g):
        for o in range(1, row):
            back_copy(s, g, o).wait_recv()

    def crossing(s, h):
        g, t = divmod(h, team)
        return back_recv[s, g, :, t].reshape(HEAD_DIM, HEAD_DIM)

    leads = [powers(h, F32(tok) - positions) for h in range(heads)]
    load(1).wait()
    load(2).wait()
    for g in range(GROUPS):
        for h in range(g * team, (g + 1) * team):
            decayed = (k_ref[:, lanes(h)].astype(F32) * leads[h]).astype(BF16)
            put_state(0, h, dot(decayed, v_ref[:, lanes(h)], 0, 0))
        if g == 0:
            pl.semaphore_wait(barrier, row + planes + peers - 3)
        start_row(0, g)
    for n in range(3, 6):
        load(n).wait()
    gain = gain_ref[...].astype(F32).reshape(1, width)

    halves = tok // HALF
    blocks = [(r, c) for r in range(halves) for c in range(r + 1)]

    def rows_of(r):
        return slice(r * HALF, (r + 1) * HALF)

    def local_forward(h):
        at = lanes(h)
        offset = (
            lax.broadcasted_iota(jnp.int32, (HALF, HALF), 0)
            - lax.broadcasted_iota(jnp.int32, (HALF, HALF), 1)
        ).astype(F32)
        rate = rates[h][0:1, :]
        for d in range(halves):
            away = offset + F32(d * HALF)
            value = jnp.exp(jnp.maximum(away, 0.0) * rate)
            if d == 0:
                value = jnp.where(away >= 0, value, 0.0)
            decay_ref[h, d] = value
        for r in range(halves):
            total = None
            for c in range(r + 1):
                scores = dot(q_ref[rows_of(r), at], k_ref[rows_of(c), at], 1, 1)
                weights = (scores * decay_ref[h, r - c]).astype(BF16)
                w_ref[h, blocks.index((r, c))] = weights
                term = dot(weights, v_ref[rows_of(c), at], 1, 0)
                total = term if total is None else total + term
            att_ref[rows_of(r), at] = total
        after = powers(h, positions + 1.0)
        dq_ref[:, at] = (q_ref[:, at].astype(F32) * after).astype(BF16)
        near_ref[:, at] = powers(h, positions)
        gg_ref[:, at] = gain[:, at] * go_ref[:, at].astype(F32)

    third = (heads + 1) // 2

    def scan(s, local):
        for h in range(third):
            local(h)
        for g in range(GROUPS):
            turn_row(s, g)
        for h in range(third, (third + heads) // 2):
            local(h)
        for g in range(GROUPS):
            turn_plane(s, g)
        for h in range((third + heads) // 2, heads):
            local(h)

    scan(0, local_forward)

    squares = jnp.zeros((tok, HEAD_DIM), F32)
    crosses = jnp.zeros((tok, HEAD_DIM), F32)
    for h in range(heads):
        at = lanes(h)
        if h % team == 0:
            end_scan(0, h // team)
        att = att_ref[:, at] + near_ref[:, at] * dot(q_ref[:, at], crossing(0, h), 1, 0)
        att_ref[:, at] = att
        squares = squares + att * att
        crosses = crosses + gg_ref[:, at] * att
    part_ref[0:1, :] = jnp.sum(squares.T, axis=0, keepdims=True)
    part_ref[1:2, :] = jnp.sum(crosses.T, axis=0, keepdims=True)

    def peer_copy(o):
        return pltpu.make_async_remote_copy(
            src_ref=part_ref,
            dst_ref=peer_recv.at[me],
            send_sem=peer_send.at[o],
            recv_sem=peer_sem.at[o],
            device_id=(seq, lax.rem(me + o, peers)),
            device_id_type=MESH,
        )

    for o in range(1, peers):
        peer_copy(o).start()
    peer_recv[me] = part_ref[...]
    for o in range(1, peers):
        peer_copy(o).wait_recv()
    sums = peer_recv[0]
    for p in range(1, peers):
        sums = sums + peer_recv[p]
    features = F32(width * peers)
    inverse_row = lax.rsqrt(sums[0:1, :] / features + EPSILON)
    mean_row = inverse_row * sums[1:2, :] / features
    inverse = jnp.broadcast_to(inverse_row, (HEAD_DIM, tok)).T
    mean = jnp.broadcast_to(mean_row, (HEAD_DIM, tok)).T

    for h in range(heads):
        at = lanes(h)
        unit = att_ref[:, at] * inverse
        grad = (inverse * (gg_ref[:, at] - unit * mean)).astype(BF16)
        ga_ref[:, at] = grad
        put_state(1, h, dot(dq_ref[:, at], grad, 0, 0))
        if h % team == team - 1:
            start_row(1, h // team)
    for h in range(heads):
        at = lanes(h)
        norm_ref[:, at] = (att_ref[:, at] * inverse * gain[:, at]).astype(BF16)
    store(0).start()

    def local_backward(h):
        at = lanes(h)
        to_q = [None] * halves
        to_k = [None] * halves
        to_v = [None] * halves

        def add(old, new):
            return new if old is None else old + new

        for r, c in blocks:
            grad = ga_ref[rows_of(r), at]
            back = dot(grad, v_ref[rows_of(c), at], 1, 1)
            back = (back * decay_ref[h, r - c]).astype(BF16)
            to_q[r] = add(to_q[r], dot(back, k_ref[rows_of(c), at], 1, 0))
            to_k[c] = add(to_k[c], dot(back, q_ref[rows_of(r), at], 0, 0))
            to_v[c] = add(to_v[c], dot(w_ref[h, blocks.index((r, c))], grad, 0, 0))
        for r in range(halves):
            near = near_ref[rows_of(r), at]
            grad = ga_ref[rows_of(r), at]
            gq_ref[rows_of(r), at] = (
                to_q[r] + near * dot(grad, crossing(0, h), 1, 1)
            ).astype(BF16)
            acck_ref[rows_of(r), at] = to_k[r].astype(BF16)
            accv_ref[rows_of(r), at] = to_v[r].astype(BF16)

    scan(1, local_backward)
    for n in range(1, 4):
        store(n).start()
    for g in range(GROUPS):
        end_scan(1, g)
        for t in range(team):
            left_ref[g * team + t] = crossing(1, g * team + t)

    for s in range(2):
        for g in range(GROUPS):
            for o in range(1, row):
                row_copy(s, g, o).wait_send()
                back_copy(s, g, o).wait_send()
            for o in range(1, planes):
                @pl.when(sends_plane(s, o))
                def _():
                    plane_copy(s, g, o).wait_send()
    for o in range(1, peers):
        peer_copy(o).wait_send()
    for n in range(4):
        store(n).wait()


def finish(codes_ref, k_ref, v_ref, left_ref, norm_in, gq_in, acck_ref, accv_ref,
           norm_ref, gq_ref, gk_ref, gv_ref):
    tok = k_ref.shape[0]
    code = jnp.full((8, HEAD_DIM), codes_ref[pl.program_id(0)], jnp.int32).astype(F32)
    rate = jnp.log1p(-jnp.exp2(-code))[0:1, :]
    positions = lax.broadcasted_iota(jnp.int32, (tok, HEAD_DIM), 0).astype(F32)
    far = jnp.exp((F32(tok - 1) - positions) * rate)
    left = left_ref[0]
    norm_ref[...] = norm_in[...]
    gq_ref[...] = gq_in[...]
    gk_ref[...] = (acck_ref[...].astype(F32) + far * dot(v_ref[...], left, 1, 1)).astype(BF16)
    gv_ref[...] = (accv_ref[...].astype(F32) + far * dot(k_ref[...], left, 1, 0)).astype(BF16)


def body(row, planes, peers, queries, keys, values, decay_codes, gain, grad_out):
    tok, width = queries.shape
    heads = width // HEAD_DIM
    part_rows = HEAD_DIM // row
    halves = tok // HALF
    team = heads // GROUPS
    slices = (team, part_rows, HEAD_DIM)
    smem = pl.BlockSpec(memory_space=pltpu.SMEM)
    vmem = pl.BlockSpec(memory_space=pltpu.VMEM)
    hbm = pl.BlockSpec(memory_space=pl.ANY)
    far = pl.BlockSpec(memory_space=pltpu.HBM)
    out = jax.ShapeDtypeStruct((tok, width), BF16)
    states = jax.ShapeDtypeStruct((heads, HEAD_DIM, HEAD_DIM), BF16)
    wide = pltpu.VMEM((tok, width), F32)
    thin = pltpu.VMEM((tok, width), BF16)
    dma = pltpu.SemaphoreType.DMA
    normalized, grad_query, key_part, value_part, left = pl.pallas_call(
        functools.partial(kernel, row, planes, peers),
        out_shape=(out,) * 4 + (states,),
        in_specs=[far] * 6,
        out_specs=(hbm,) * 4 + (vmem,),
        scratch_shapes=[pltpu.SMEM((heads,), jnp.int32), pltpu.VMEM((width,), BF16)] + [thin] * 8 + [
            pltpu.VMEM((heads, halves, HALF, HALF), F32),
            pltpu.VMEM((heads, halves * (halves + 1) // 2, HALF, HALF), BF16),
            wide, wide, thin, thin, wide,
            pltpu.VMEM((2, GROUPS, row) + slices, BF16),
            pltpu.VMEM((2, GROUPS, row) + slices, BF16),
            pltpu.VMEM((2, GROUPS, row) + slices, F32),
            pltpu.VMEM((2, GROUPS) + slices, BF16),
            pltpu.VMEM((2, GROUPS, planes) + slices, BF16),
            pltpu.VMEM((2, GROUPS, row) + slices, BF16),
            pltpu.VMEM((2, GROUPS, row) + slices, BF16),
            pltpu.VMEM((2, tok), F32),
            pltpu.VMEM((peers, 2, tok), F32),
            dma((6,)),
            dma((4,)),
            dma((2 * GROUPS, row)),
            dma((2 * GROUPS, row)),
            dma((2 * GROUPS, planes)),
            dma((2 * GROUPS, planes)),
            dma((2 * GROUPS, row)),
            dma((2 * GROUPS, row)),
            dma((peers,)),
            dma((peers,)),
        ],
        compiler_params=pltpu.CompilerParams(
            collective_id=0, has_side_effects=True, vmem_limit_bytes=VMEM_A
        ),
        name="lightning",
    )(decay_codes, queries, keys, values, gain, grad_out)
    column = pl.BlockSpec((tok, HEAD_DIM), lambda h: (0, h))
    return pl.pallas_call(
        finish,
        grid=(heads,),
        out_shape=(out,) * 4,
        in_specs=[smem, column, column, pl.BlockSpec((1, HEAD_DIM, HEAD_DIM), lambda h: (h, 0, 0))]
        + [column] * 4,
        out_specs=(column,) * 4,
        compiler_params=pltpu.CompilerParams(vmem_limit_bytes=VMEM_B),
        name="finish",
    )(decay_codes, keys, values, left, normalized, grad_query, key_part, value_part)


def solution(mesh):
    split = P("seq", "head")
    planes = mesh.shape["seq"] // ROW
    return jax.shard_map(
        functools.partial(body, ROW, planes, mesh.shape["head"]),
        mesh=mesh,
        in_specs=(split, split, split, P("head"), P("head"), split),
        out_specs=(split,) * 4,
        check_vma=False,
    )
```

time: 63.3 us -> 57.6 us (0.910)
  the two profiles are of different devices: /device:TPU:16 before, /device:TPU:1 now
where the time goes in v2:
time: 57.6 us; the launch traced here: 56.7 us
  Pallas kernels  56.1 us (97%)
  between operations  0.64 us (1%)
    pallas_call x1, Pallas kernels, body(): pl.pallas_call(functools.partial(kernel, row, planes, peers), out_shape=(...  51.7 us
    pallas_call x1, Pallas kernels, body(): pl.pallas_call(finish, grid=(heads,), out_shape=(out,) * 4, in_specs=[sme...  4.39 us

profile of v2, /device:TPU:1, one launch (start us, length us, event | category | flops | bytes accessed | tf_op | source)
XLA Modules:
  0.0 56.7 jit_solution(5843876521027586621)
XLA Ops:
  0.6 51.7 %lightning.1 = (bf16[512,512]{1,0:T(8,128)(2,1)}, bf16[512,512]{1,0:T(8,128)(2,1)}, bf16[512,512]{1,0:T(8,128)(2,1)}, bf16[512,512]{1,0:T(8,128)(2,1)}, bf16[4,128,128]{2,1,0:T(8,128)(2,1)}) custom-call(s32[4]{0:T(128)} %codes_ref.1, bf16[512,512]{1,0:T(8,128)(2,1)} %q_hbm.1, bf16[512,512]{1,0:T(8,128)(2,1)} %k_ref.1, bf16[512,512]{1,0:T(8,128)(2,1)} %v_ref.1, ...), custom_call_target="tpu_custom_call" | custom-call | tf_op jit(solution)/shard_map/lightning/pallas_call | solution.py:376
  52.3 4.4 %finish.1 = (bf16[512,512]{1,0:T(8,128)(2,1)}, bf16[512,512]{1,0:T(8,128)(2,1)}, bf16[512,512]{1,0:T(8,128)(2,1)}, bf16[512,512]{1,0:T(8,128)(2,1)}) custom-call(s32[4]{0:T(128)} %codes_ref.1, bf16[512,512]{1,0:T(8,128)(2,1)} %k_ref.1, bf16[512,512]{1,0:T(8,128)(2,1)} %v_ref.1, bf16[4,128,128]{2,1,0:T(8,128)(2,1)} %get-tuple-element.9.left_ref, ...), custom_call_target="tpu_custom_call" | custom-call | tf_op jit(solution)/shard_map/finish/pallas_call | solution.py:411

commit v3 on v2

--- a/solution.py
+++ b/solution.py
@@ -12,8 +12,8 @@
 ROW = 8
 HALF = 256
 GROUPS = 2
-VMEM_A = 67043328
-VMEM_B = 67043328
+VMEM_A = 62600000
+VMEM_B = 16777216
 F32 = jnp.float32
 BF16 = jnp.bfloat16
 MESH = pl.DeviceIdType.MESH
@@ -26,11 +26,11 @@
 def kernel(
     row, planes, peers,
     codes_hbm, q_hbm, k_hbm, v_hbm, gain_hbm, go_hbm,
-    norm_out, gq_out, acck_out, accv_out, left_ref,
-    codes_ref, gain_ref, q_ref, k_ref, v_ref, go_ref, norm_ref, gq_ref, acck_ref, accv_ref,
+    norm_ref, gq_ref, acck_ref, accv_ref, left_ref, k_ref, v_ref, far_ref,
+    codes_ref, gain_ref, q_ref, go_ref,
     decay_ref, w_ref, att_ref, gg_ref, ga_ref, dq_ref, near_ref,
     state_ref, row_recv, pre_ref, tot_ref, plane_recv, full_ref, back_recv,
-    part_ref, peer_recv, load_sem, store_sem,
+    part_ref, peer_recv, load_sem,
     row_send, row_sem, plane_send, plane_sem, back_send, back_sem, peer_send, peer_sem,
 ):
     tok, width = q_ref.shape
@@ -48,13 +48,9 @@
         (codes_hbm, codes_ref), (k_hbm, k_ref), (v_hbm, v_ref),
         (q_hbm, q_ref), (gain_hbm, gain_ref), (go_hbm, go_ref),
     )
-    results = ((norm_ref, norm_out), (gq_ref, gq_out), (acck_ref, acck_out), (accv_ref, accv_out))
 
     def load(n):
         return pltpu.make_async_copy(*sources[n], load_sem.at[n])
-
-    def store(n):
-        return pltpu.make_async_copy(*results[n], store_sem.at[n])
 
     for n in range(6):
         load(n).start()
@@ -227,6 +223,7 @@
         after = powers(h, positions + 1.0)
         dq_ref[:, at] = (q_ref[:, at].astype(F32) * after).astype(BF16)
         near_ref[:, at] = powers(h, positions)
+        far_ref[:, at] = powers(h, F32(tok - 1) - positions)
         gg_ref[:, at] = gain[:, at] * go_ref[:, at].astype(F32)
 
     third = (heads + 1) // 2
@@ -293,7 +290,6 @@
     for h in range(heads):
         at = lanes(h)
         norm_ref[:, at] = (att_ref[:, at] * inverse * gain[:, at]).astype(BF16)
-    store(0).start()
 
     def local_backward(h):
         at = lanes(h)
@@ -321,8 +317,6 @@
             accv_ref[rows_of(r), at] = to_v[r].astype(BF16)
 
     scan(1, local_backward)
-    for n in range(1, 4):
-        store(n).start()
     for g in range(GROUPS):
         end_scan(1, g)
         for t in range(team):
@@ -339,22 +333,37 @@
                     plane_copy(s, g, o).wait_send()
     for o in range(1, peers):
         peer_copy(o).wait_send()
-    for n in range(4):
-        store(n).wait()
-
-
-def finish(codes_ref, k_ref, v_ref, left_ref, norm_in, gq_in, acck_ref, accv_ref,
-           norm_ref, gq_ref, gk_ref, gv_ref):
-    tok = k_ref.shape[0]
-    code = jnp.full((8, HEAD_DIM), codes_ref[pl.program_id(0)], jnp.int32).astype(F32)
-    rate = jnp.log1p(-jnp.exp2(-code))[0:1, :]
-    positions = lax.broadcasted_iota(jnp.int32, (tok, HEAD_DIM), 0).astype(F32)
-    far = jnp.exp((F32(tok - 1) - positions) * rate)
-    left = left_ref[0]
-    norm_ref[...] = norm_in[...]
-    gq_ref[...] = gq_in[...]
-    gk_ref[...] = (acck_ref[...].astype(F32) + far * dot(v_ref[...], left, 1, 1)).astype(BF16)
-    gv_ref[...] = (accv_ref[...].astype(F32) + far * dot(k_ref[...], left, 1, 0)).astype(BF16)
+
+
+def finish(k_ref, v_ref, left_ref, norm_ref, gq_ref, acck_ref, accv_ref, far_ref,
+           norm_out, gq_out, gk_out, gv_out, gk_ref, gv_ref, store_sem, part_sem):
+    stores = [
+        pltpu.make_async_copy(norm_ref, norm_out, store_sem.at[0]),
+        pltpu.make_async_copy(gq_ref, gq_out, store_sem.at[1]),
+    ]
+    for store in stores:
+        store.start()
+    heads = left_ref.shape[0]
+    for h in range(heads):
+        at = slice(h * HEAD_DIM, (h + 1) * HEAD_DIM)
+        far, left = far_ref[:, at], left_ref[h]
+        gk_ref[:, at] = (
+            acck_ref[:, at].astype(F32) + far * dot(v_ref[:, at], left, 1, 1)
+        ).astype(BF16)
+        gv_ref[:, at] = (
+            accv_ref[:, at].astype(F32) + far * dot(k_ref[:, at], left, 1, 0)
+        ).astype(BF16)
+        if h % 2 == 1:
+            both = slice((h - 1) * HEAD_DIM, (h + 1) * HEAD_DIM)
+            for n, (src, dst) in enumerate(((gk_ref, gk_out), (gv_ref, gv_out))):
+                stores.append(
+                    pltpu.make_async_copy(
+                        src.at[:, both], dst.at[:, both], part_sem.at[n, h // 2]
+                    )
+                )
+                stores[-1].start()
+    for store in stores:
+        store.wait()
 
 
 def body(row, planes, peers, queries, keys, values, decay_codes, gain, grad_out):
@@ -364,21 +373,18 @@
     halves = tok // HALF
     team = heads // GROUPS
     slices = (team, part_rows, HEAD_DIM)
-    smem = pl.BlockSpec(memory_space=pltpu.SMEM)
     vmem = pl.BlockSpec(memory_space=pltpu.VMEM)
-    hbm = pl.BlockSpec(memory_space=pl.ANY)
     far = pl.BlockSpec(memory_space=pltpu.HBM)
     out = jax.ShapeDtypeStruct((tok, width), BF16)
-    states = jax.ShapeDtypeStruct((heads, HEAD_DIM, HEAD_DIM), BF16)
     wide = pltpu.VMEM((tok, width), F32)
     thin = pltpu.VMEM((tok, width), BF16)
     dma = pltpu.SemaphoreType.DMA
-    normalized, grad_query, key_part, value_part, left = pl.pallas_call(
+    normalized, grad_query, key_part, value_part, left, near_keys, near_values, far_powers = pl.pallas_call(
         functools.partial(kernel, row, planes, peers),
-        out_shape=(out,) * 4 + (states,),
+        out_shape=(thin,) * 4 + (pltpu.VMEM((heads, HEAD_DIM, HEAD_DIM), BF16), thin, thin, wide),
         in_specs=[far] * 6,
-        out_specs=(hbm,) * 4 + (vmem,),
-        scratch_shapes=[pltpu.SMEM((heads,), jnp.int32), pltpu.VMEM((width,), BF16)] + [thin] * 8 + [
+        out_specs=(vmem,) * 8,
+        scratch_shapes=[pltpu.SMEM((heads,), jnp.int32), pltpu.VMEM((width,), BF16)] + [thin] * 2 + [
             pltpu.VMEM((heads, halves, HALF, HALF), F32),
             pltpu.VMEM((heads, halves * (halves + 1) // 2, HALF, HALF), BF16),
             wide, wide, thin, thin, wide,
@@ -392,7 +398,6 @@
             pltpu.VMEM((2, tok), F32),
             pltpu.VMEM((peers, 2, tok), F32),
             dma((6,)),
-            dma((4,)),
             dma((2 * GROUPS, row)),
             dma((2 * GROUPS, row)),
             dma((2 * GROUPS, planes)),
@@ -407,17 +412,15 @@
         ),
         name="lightning",
     )(decay_codes, queries, keys, values, gain, grad_out)
-    column = pl.BlockSpec((tok, HEAD_DIM), lambda h: (0, h))
     return pl.pallas_call(
         finish,
-        grid=(heads,),
         out_shape=(out,) * 4,
-        in_specs=[smem, column, column, pl.BlockSpec((1, HEAD_DIM, HEAD_DIM), lambda h: (h, 0, 0))]
-        + [column] * 4,
-        out_specs=(column,) * 4,
+        in_specs=[vmem] * 8,
+        out_specs=(far,) * 4,
+        scratch_shapes=[thin, thin, dma((2,)), dma((2, heads // 2))],
         compiler_params=pltpu.CompilerParams(vmem_limit_bytes=VMEM_B),
         name="finish",
-    )(decay_codes, keys, values, left, normalized, grad_query, key_part, value_part)
+    )(near_keys, near_values, left, normalized, grad_query, key_part, value_part, far_powers)
 
 
 def solution(mesh):

time: 57.6 us -> 53.9 us (0.936)
  Pallas kernels: 56.1 us -> 52.4 us
    pallas_call x1, Pallas kernels: 4.39 us -> 1.47 us  [body(): pl.pallas_call(finish, out_shape=(out,) * 4, in_specs=[vmem] * 8, out_spe...]
    pallas_call x1, Pallas kernels: 51.7 us -> 50.9 us  [body(): pl.pallas_call(functools.partial(kernel, row, planes, peers), out_shape=(...]
where the time goes in v3:
time: 53.9 us; the launch traced here: 53 us
  Pallas kernels  52.4 us (97%)
  between operations  0.64 us (1%)
    pallas_call x1, Pallas kernels, body(): pl.pallas_call(functools.partial(kernel, row, planes, peers), out_shape=(...  50.9 us
    pallas_call x1, Pallas kernels, body(): pl.pallas_call(finish, out_shape=(out,) * 4, in_specs=[vmem] * 8, out_spe...  1.47 us

profile of v3, /device:TPU:1, one launch (start us, length us, event | category | flops | bytes accessed | tf_op | source)
XLA Modules:
  0.0 53.0 jit_solution(9810887011861618977)
XLA Ops:
  0.6 50.9 %lightning.1 = (bf16[512,512]{1,0:T(8,128)(2,1)S(1)}, bf16[512,512]{1,0:T(8,128)(2,1)S(1)}, bf16[512,512]{1,0:T(8,128)(2,1)S(1)}, bf16[512,512]{1,0:T(8,128)(2,1...) custom-call(s32[4]{0:T(128)} %codes_hbm.1, ...), custom_call_target="tpu_custom_call" | custom-call | tf_op jit(solution)/shard_map/lightning/pallas_call | solution.py:382
  51.6 1.5 %finish.1 = (bf16[512,512]{1,0:T(8,128)(2,1)}, bf16[512,512]{1,0:T(8,128)(2,1)}, bf16[512,512]{1,0:T(8,128)(2,1)}, bf16[512,512]{1,0:T(8,128)(2,1)}) custom-call(bf16[512,512]{1,0:T(8,128)(2,1)S(1)} %get-tuple-element.12.k_ref, bf16[512,512]{1,0:T(8,128)(2,1)S(1)} %get-tuple-element.13.v_ref, bf16[4,128,128]{2,1,0:T(8,128)(2,1)S(1)} %get-tuple-element.14.left_ref, ...), custom_call_target="tpu_custom_call" | custom-call | tf_op jit(solution)/shard_map/finish/pallas_call | solution.py:415

commit v4 on v3

--- a/solution.py
+++ b/solution.py
@@ -17,6 +17,10 @@
 F32 = jnp.float32
 BF16 = jnp.bfloat16
 MESH = pl.DeviceIdType.MESH
+
+
+def others(count):
+    return sorted(range(1, count), key=lambda o: -min(o, count - o))
 
 
 def dot(a, b, ca, cb):
@@ -52,22 +56,22 @@
     def load(n):
         return pltpu.make_async_copy(*sources[n], load_sem.at[n])
 
+    barrier = pltpu.get_barrier_semaphore()
+    for o in others(row):
+        pl.semaphore_signal(
+            barrier, inc=1, device_id=(z * row + row_peer(o), me), device_id_type=MESH
+        )
+    for o in others(planes):
+        pl.semaphore_signal(
+            barrier, inc=1, device_id=(lax.rem(z + o, planes) * row + y, me), device_id_type=MESH
+        )
+    for o in others(peers):
+        pl.semaphore_signal(
+            barrier, inc=1, device_id=(seq, lax.rem(me + o, peers)), device_id_type=MESH
+        )
+
     for n in range(6):
         load(n).start()
-
-    barrier = pltpu.get_barrier_semaphore()
-    for o in range(1, row):
-        pl.semaphore_signal(
-            barrier, inc=1, device_id=(z * row + row_peer(o), me), device_id_type=MESH
-        )
-    for o in range(1, planes):
-        pl.semaphore_signal(
-            barrier, inc=1, device_id=(lax.rem(z + o, planes) * row + y, me), device_id_type=MESH
-        )
-    for o in range(1, peers):
-        pl.semaphore_signal(
-            barrier, inc=1, device_id=(seq, lax.rem(me + o, peers)), device_id_type=MESH
-        )
 
     def lanes(h):
         return slice(h * HEAD_DIM, (h + 1) * HEAD_DIM)
@@ -128,12 +132,12 @@
         state_ref[s, g, :, t] = value.astype(BF16).reshape(row, part_rows, HEAD_DIM)
 
     def start_row(s, g):
-        for o in range(1, row):
+        for o in others(row):
             row_copy(s, g, o).start()
         row_recv[s, g, y] = state_ref[s, g, y]
 
     def turn_row(s, g):
-        for o in range(1, row):
+        for o in others(row):
             row_copy(s, g, o).wait_recv()
         for t in range(team):
             step = power(g * team + t, tok)
@@ -142,13 +146,13 @@
                 pre_ref[s, g, c, t] = held
                 held = step * held + row_recv[s, g, c, t].astype(F32)
             tot_ref[s, g, t] = held.astype(BF16)
-        for o in range(1, planes):
+        for o in others(planes):
             @pl.when(sends_plane(s, o))
             def _():
                 plane_copy(s, g, o).start()
 
     def turn_plane(s, g):
-        for o in range(1, planes):
+        for o in others(planes):
             @pl.when(takes_plane(s, o))
             def _():
                 plane_copy(s, g, o).wait_recv()
@@ -166,12 +170,12 @@
             for c in range(row):
                 far = power(g * team + t, tok * (c if s == 0 else row - 1 - c))
                 full_ref[s, g, c, t] = (pre_ref[s, g, c, t] + far * held[t]).astype(BF16)
-        for o in range(1, row):
+        for o in others(row):
             back_copy(s, g, o).start()
         back_recv[s, g, y] = full_ref[s, g, y]
 
     def end_scan(s, g):
-        for o in range(1, row):
+        for o in others(row):
             back_copy(s, g, o).wait_recv()
 
     def crossing(s, h):
@@ -221,7 +225,7 @@
                 total = term if total is None else total + term
             att_ref[rows_of(r), at] = total
         after = powers(h, positions + 1.0)
-        dq_ref[:, at] = (q_ref[:, at].astype(F32) * after).astype(BF16)
+        dq_ref[h] = (q_ref[:, at].astype(F32) * after).astype(BF16).T
         near_ref[:, at] = powers(h, positions)
         far_ref[:, at] = powers(h, F32(tok - 1) - positions)
         gg_ref[:, at] = gain[:, at] * go_ref[:, at].astype(F32)
@@ -265,10 +269,10 @@
             device_id_type=MESH,
         )
 
-    for o in range(1, peers):
+    for o in others(peers):
         peer_copy(o).start()
     peer_recv[me] = part_ref[...]
-    for o in range(1, peers):
+    for o in others(peers):
         peer_copy(o).wait_recv()
     sums = peer_recv[0]
     for p in range(1, peers):
@@ -284,7 +288,7 @@
         unit = att_ref[:, at] * inverse
         grad = (inverse * (gg_ref[:, at] - unit * mean)).astype(BF16)
         ga_ref[:, at] = grad
-        put_state(1, h, dot(dq_ref[:, at], grad, 0, 0))
+        put_state(1, h, dot(dq_ref[h], grad, 1, 0))
         if h % team == team - 1:
             start_row(1, h // team)
     for h in range(heads):
@@ -324,14 +328,14 @@
 
     for s in range(2):
         for g in range(GROUPS):
-            for o in range(1, row):
+            for o in others(row):
                 row_copy(s, g, o).wait_send()
                 back_copy(s, g, o).wait_send()
-            for o in range(1, planes):
+            for o in others(planes):
                 @pl.when(sends_plane(s, o))
                 def _():
                     plane_copy(s, g, o).wait_send()
-    for o in range(1, peers):
+    for o in others(peers):
         peer_copy(o).wait_send()
 
 
@@ -387,7 +391,7 @@
         scratch_shapes=[pltpu.SMEM((heads,), jnp.int32), pltpu.VMEM((width,), BF16)] + [thin] * 2 + [
             pltpu.VMEM((heads, halves, HALF, HALF), F32),
             pltpu.VMEM((heads, halves * (halves + 1) // 2, HALF, HALF), BF16),
-            wide, wide, thin, thin, wide,
+            wide, wide, thin, pltpu.VMEM((heads, HEAD_DIM, tok), BF16), wide,
             pltpu.VMEM((2, GROUPS, row) + slices, BF16),
             pltpu.VMEM((2, GROUPS, row) + slices, BF16),
             pltpu.VMEM((2, GROUPS, row) + slices, F32),

time: 53.9 us -> 52 us (0.965)
  Pallas kernels: 52.4 us -> 50.6 us
    pallas_call x1, Pallas kernels: 50.9 us -> 49.1 us  [body(): pl.pallas_call(functools.partial(kernel, row, planes, peers), out_shape=(...]
where the time goes in v4:
time: 52 us; the launch traced here: 51.2 us
  Pallas kernels  50.6 us (97%)
  between operations  0.64 us (1%)
    pallas_call x1, Pallas kernels, body(): pl.pallas_call(functools.partial(kernel, row, planes, peers), out_shape=(...  49.1 us
    pallas_call x1, Pallas kernels, body(): pl.pallas_call(finish, out_shape=(out,) * 4, in_specs=[vmem] * 8, out_spe...  1.47 us

profile of v4, /device:TPU:1, one launch (start us, length us, event | category | flops | bytes accessed | tf_op | source)
XLA Modules:
  0.0 51.2 jit_solution(11492926780806800334)
XLA Ops:
  0.6 49.1 %lightning.1 = (bf16[512,512]{1,0:T(8,128)(2,1)S(1)}, bf16[512,512]{1,0:T(8,128)(2,1)S(1)}, bf16[512,512]{1,0:T(8,128)(2,1)S(1)}, bf16[512,512]{1,0:T(8,128)(2,1...) custom-call(s32[4]{0:T(128)} %codes_hbm.1, ...), custom_call_target="tpu_custom_call" | custom-call | tf_op jit(solution)/shard_map/lightning/pallas_call | solution.py:386
  49.8 1.5 %finish.1 = (bf16[512,512]{1,0:T(8,128)(2,1)}, bf16[512,512]{1,0:T(8,128)(2,1)}, bf16[512,512]{1,0:T(8,128)(2,1)}, bf16[512,512]{1,0:T(8,128)(2,1)}) custom-call(bf16[512,512]{1,0:T(8,128)(2,1)S(1)} %get-tuple-element.12.k_ref, bf16[512,512]{1,0:T(8,128)(2,1)S(1)} %get-tuple-element.13.v_ref, bf16[4,128,128]{2,1,0:T(8,128)(2,1)S(1)} %get-tuple-element.14.left_ref, ...), custom_call_target="tpu_custom_call" | custom-call | tf_op jit(solution)/shard_map/finish/pallas_call | solution.py:419

commit v5 on v4

--- a/solution.py
+++ b/solution.py
@@ -137,14 +137,14 @@
         row_recv[s, g, y] = state_ref[s, g, y]
 
     def turn_row(s, g):
+        steps = [power(g * team + t, tok) for t in range(team)]
         for o in others(row):
             row_copy(s, g, o).wait_recv()
         for t in range(team):
-            step = power(g * team + t, tok)
             held = jnp.zeros((part_rows, HEAD_DIM), F32)
             for c in range(row) if s == 0 else reversed(range(row)):
                 pre_ref[s, g, c, t] = held
-                held = step * held + row_recv[s, g, c, t].astype(F32)
+                held = steps[t] * held + row_recv[s, g, c, t].astype(F32)
             tot_ref[s, g, t] = held.astype(BF16)
         for o in others(planes):
             @pl.when(sends_plane(s, o))
@@ -152,12 +152,16 @@
                 plane_copy(s, g, o).start()
 
     def turn_plane(s, g):
+        leap = [power(g * team + t, tok * row) for t in range(team)]
+        fars = [
+            [power(g * team + t, tok * (c if s == 0 else row - 1 - c)) for c in range(row)]
+            for t in range(team)
+        ]
         for o in others(planes):
             @pl.when(takes_plane(s, o))
             def _():
                 plane_copy(s, g, o).wait_recv()
         zero = tuple(jnp.zeros((part_rows, HEAD_DIM), F32) for _ in range(team))
-        leap = [power(g * team + t, tok * row) for t in range(team)]
 
         def add(n, held):
             at = n if s == 0 else planes - 1 - n
@@ -168,8 +172,7 @@
         held = lax.fori_loop(0, z if s == 0 else planes - 1 - z, add, zero)
         for t in range(team):
             for c in range(row):
-                far = power(g * team + t, tok * (c if s == 0 else row - 1 - c))
-                full_ref[s, g, c, t] = (pre_ref[s, g, c, t] + far * held[t]).astype(BF16)
+                full_ref[s, g, c, t] = (pre_ref[s, g, c, t] + fars[t][c] * held[t]).astype(BF16)
         for o in others(row):
             back_copy(s, g, o).start()
         back_recv[s, g, y] = full_ref[s, g, y]

time: 52 us -> 52 us (level)
  no operation moved by 1% of the time
where the time goes in v5:
time: 52 us; the launch traced here: 51.2 us
  Pallas kernels  50.6 us (97%)
  between operations  0.64 us (1%)
    pallas_call x1, Pallas kernels, body(): pl.pallas_call(functools.partial(kernel, row, planes, peers), out_shape=(...  49.1 us
    pallas_call x1, Pallas kernels, body(): pl.pallas_call(finish, out_shape=(out,) * 4, in_specs=[vmem] * 8, out_spe...  1.47 us

profile of v5, /device:TPU:1, one launch (start us, length us, event | category | flops | bytes accessed | tf_op | source)
XLA Modules:
  0.0 51.2 jit_solution(8986543526624701534)
XLA Ops:
  0.6 49.1 %lightning.1 = (bf16[512,512]{1,0:T(8,128)(2,1)S(1)}, bf16[512,512]{1,0:T(8,128)(2,1)S(1)}, bf16[512,512]{1,0:T(8,128)(2,1)S(1)}, bf16[512,512]{1,0:T(8,128)(2,1...) custom-call(s32[4]{0:T(128)} %codes_hbm.1, ...), custom_call_target="tpu_custom_call" | custom-call | tf_op jit(solution)/shard_map/lightning/pallas_call | solution.py:389
  49.7 1.5 %finish.1 = (bf16[512,512]{1,0:T(8,128)(2,1)}, bf16[512,512]{1,0:T(8,128)(2,1)}, bf16[512,512]{1,0:T(8,128)(2,1)}, bf16[512,512]{1,0:T(8,128)(2,1)}) custom-call(bf16[512,512]{1,0:T(8,128)(2,1)S(1)} %get-tuple-element.12.k_ref, bf16[512,512]{1,0:T(8,128)(2,1)S(1)} %get-tuple-element.13.v_ref, bf16[4,128,128]{2,1,0:T(8,128)(2,1)S(1)} %get-tuple-element.14.left_ref, ...), custom_call_target="tpu_custom_call" | custom-call | tf_op jit(solution)/shard_map/finish/pallas_call | solution.py:422
